TPU v7x, 128 devices: a whole 4x4x4 slice. The times are simulated.
128 devices in a mesh: seq: 16 (over z, y_lo, core), head: 8 (over x, y_hi).
Axes of the slice: x: 4, y: 4 (y_hi: 2, y_lo: 2; y = y_hi * 2 + y_lo), z: 4, core: 2. Of those that a mesh axis runs over, the one named last changes fastest.
Arguments:
- tokens: bfloat16 [128, 512, 1024], P('seq'), may hold values from -36 to 36
- lengths: int32 [128], P('seq'), may hold values from 1 to 512, 32768 in all
- attn_in: float32 [1024, 3, 1024], P(('seq', 'head')), may hold values from -0.4 to 0.4
- attn_out: float32 [1024, 1024], P(None, ('seq', 'head')), may hold values from -0.1875 to 0.1875
- mlp_in: float32 [1024, 4096], P(('seq', 'head')), may hold values from -0.1875 to 0.1875
- mlp_out: float32 [4096, 1024], P(None, ('seq', 'head')), may hold values from -0.09375 to 0.09375
- norm_gain: float32 [2, 1024], replicated, may hold values from 0.5 to 1.5
- norm_shift: float32 [2, 1024], replicated, may hold values from -3 to 3
Outputs:
- encoded: bfloat16 [128, 512, 1024], P('seq', 'head')
- key_cache: bfloat16 [128, 512, 1024], P('seq', None, 'head')
- value_cache: bfloat16 [128, 512, 1024], P('seq', None, 'head')
Inputs may be any that keep to these rules, and one draw needn't show every extreme that they name: `lengths`: some prompt has exactly 512 tokens.
All inputs are finite; a program needn't handle non-finite values. No bound on the sum of `lengths` on one device may be relied on, other than what follows from the above.
Results may differ from a plain program's by a relative error of at most 0.02.
Values may be sent and summed in bfloat16 or wider, within the bound.
A program may use at most 128 MiB of HBM per device.

v0:
```python
import math
import jax
import jax.numpy as jnp
from jax import lax
from jax.sharding import PartitionSpec as P

DH = 64
EPSILON = 1e-05
CHUNKS = 1


def layer_norm(values, gain, shift):
    center = values - jnp.mean(values, axis=-1, keepdims=True)
    spread = jnp.mean(center * center, axis=-1, keepdims=True)
    return center * lax.rsqrt(spread + EPSILON) * gain + shift


def regroup_weights(attn_in, attn_out, mlp_in, mlp_out, heads_axis, seq_axis):
    rows = attn_in.shape[0]
    model_width = attn_in.shape[2]
    hidden_width = mlp_in.shape[1]
    block_width = model_width // heads_axis
    in_piece = attn_in.astype(jnp.bfloat16).reshape(rows, 3, heads_axis, block_width)
    in_piece = jnp.transpose(in_piece, (0, 2, 1, 3)).reshape(rows, heads_axis, 3 * block_width)
    whole_rows = jnp.concatenate(
        [
            attn_out.astype(jnp.bfloat16).T,
            mlp_in.astype(jnp.bfloat16),
            mlp_out.astype(jnp.bfloat16).T,
        ],
        axis=1,
    )
    whole_piece = jnp.broadcast_to(whole_rows[:, None], (rows, heads_axis, whole_rows.shape[1]))
    packed = jnp.concatenate([in_piece, whole_piece], axis=2)
    packed = lax.all_to_all(packed, "head", 1, 0, tiled=True)
    packed = packed.reshape(rows * heads_axis, packed.shape[2])
    in_part = packed[:, : 3 * block_width]
    in_part = jnp.broadcast_to(in_part[None], (seq_axis,) + in_part.shape)
    qkv_weight = lax.all_to_all(in_part, "seq", 0, 0, tiled=True)
    qkv_weight = qkv_weight.reshape(-1, 3, block_width)
    early_end = 3 * block_width + model_width + hidden_width
    early = lax.all_gather(packed[:, 3 * block_width : early_end], "seq", axis=0, tiled=True)
    proj_weight_t = early[:, :model_width]
    up_weight = early[:, model_width:]
    down_weight_t = lax.all_gather(packed[:, early_end:], "seq", axis=0, tiled=True)
    return (qkv_weight, proj_weight_t, up_weight, down_weight_t)


def encode_chunk(
    tokens,
    lengths,
    qkv_weight,
    proj_weight_t,
    up_weight,
    down_weight_t,
    norm_gain,
    norm_shift,
    heads_axis,
    head_index,
):
    prompts = tokens.shape[0]
    seq_len = tokens.shape[1]
    model_width = tokens.shape[2]
    hidden_width = up_weight.shape[1]
    block_width = model_width // heads_axis
    hidden_block = hidden_width // heads_axis
    local_heads = block_width // DH
    row_count = seq_len // heads_axis
    row_start = head_index * row_count
    projected = jnp.einsum(
        "pld,dte->plte", tokens, qkv_weight, preferred_element_type=jnp.float32
    ).astype(jnp.bfloat16)
    positions = jnp.arange(seq_len, dtype=jnp.int32)
    inside = positions[None, :] < lengths[:, None]
    key_part = projected[:, :, 1]
    value_part = projected[:, :, 2]
    queries = projected[:, :, 0].reshape(prompts, seq_len, local_heads, DH)
    key_heads = key_part.reshape(prompts, seq_len, local_heads, DH)
    value_heads = value_part.reshape(prompts, seq_len, local_heads, DH)
    scores = jnp.einsum(
        "pqhd,pkhd->phqk", queries, key_heads, preferred_element_type=jnp.float32
    ) * (1.0 / math.sqrt(DH))
    scores = jnp.where(inside[:, None, None, :], scores, -1e30)
    row_peak = jnp.max(scores, axis=-1, keepdims=True)
    raised = jnp.exp(scores - row_peak)
    weights = (raised / jnp.sum(raised, axis=-1, keepdims=True)).astype(jnp.bfloat16)
    context = jnp.einsum(
        "phqk,pkhd->pqhd", weights, value_heads, preferred_element_type=jnp.float32
    )
    context = context.astype(jnp.bfloat16).reshape(prompts, heads_axis, row_count, block_width)
    key_cache = jnp.where(inside[:, :, None], key_part, jnp.zeros_like(key_part))
    value_cache = jnp.where(inside[:, :, None], value_part, jnp.zeros_like(value_part))
    context_blocks = jnp.transpose(context, (1, 0, 2, 3))
    context_blocks = lax.all_to_all(context_blocks, "head", 0, 0, tiled=True)
    proj_blocks = proj_weight_t.reshape(model_width, heads_axis, block_width)
    attn_rows = jnp.einsum(
        "sprf,esf->pre", context_blocks, proj_blocks, preferred_element_type=jnp.float32
    )
    token_rows = lax.dynamic_slice_in_dim(tokens, row_start, row_count, 1)
    normed_rows = layer_norm(
        token_rows.astype(jnp.float32) + attn_rows, norm_gain[0], norm_shift[0]
    ).astype(jnp.bfloat16)
    hidden = jax.nn.gelu(
        jnp.einsum("pld,df->plf", normed_rows, up_weight, preferred_element_type=jnp.float32),
        approximate=False,
    ).astype(jnp.bfloat16)
    hidden = lax.optimization_barrier(hidden)
    mlp_rows = jnp.einsum("plf,ef->ple", hidden, down_weight_t, preferred_element_type=jnp.float32)
    finished = layer_norm(normed_rows.astype(jnp.float32) + mlp_rows, norm_gain[1], norm_shift[1])
    inside_rows = lax.dynamic_slice_in_dim(inside, row_start, row_count, 1)
    encoded = jnp.where(inside_rows[:, :, None], finished, 0.0).astype(jnp.bfloat16)
    return (encoded, key_cache, value_cache)


def shards(tokens, lengths, attn_in, attn_out, mlp_in, mlp_out, norm_gain, norm_shift):
    heads_axis = lax.axis_size("head")
    head_index = lax.axis_index("head")
    qkv_weight, proj_weight_t, up_weight, down_weight_t = regroup_weights(
        attn_in, attn_out, mlp_in, mlp_out, heads_axis, lax.axis_size("seq")
    )
    prompts = tokens.shape[0]
    chunk = max(1, prompts // CHUNKS)
    pieces = []
    for lower in range(0, prompts, chunk):
        pieces.append(
            encode_chunk(
                tokens[lower : lower + chunk],
                lengths[lower : lower + chunk],
                qkv_weight,
                proj_weight_t,
                up_weight,
                down_weight_t,
                norm_gain,
                norm_shift,
                heads_axis,
                head_index,
            )
        )
    return tuple((jnp.concatenate(parts, axis=0) for parts in zip(*pieces)))


def solution(mesh):
    in_specs = (
        P("seq", None, None),
        P("seq"),
        P(("seq", "head"), None, None),
        P(None, ("seq", "head")),
        P(("seq", "head"), None),
        P(None, ("seq", "head")),
        P(),
        P(),
    )
    out_specs = (P("seq", "head", None), P("seq", None, "head"), P("seq", None, "head"))
    return jax.shard_map(shards, mesh=mesh, in_specs=in_specs, out_specs=out_specs, check_vma=False)
```

profile of v0, /device:TPU:25, one launch (start us, length us, event | category | flops | bytes accessed | tf_op | source)
XLA Modules:
  0.0 181.5 jit_solution(4619803239640551789)
XLA Ops:
  7.2 0.0 copy-start.3
  7.2 0.0 all-gather.3.cloned.1.call-start
  7.2 0.9 convert_bitcast_fusion.1
  8.1 0.9 convert_element_type.45
  9.0 0.8 convert_bitcast_fusion.3
  9.8 0.9 copy_bitcast_fusion
  10.7 0.1 broadcast_in_dim.36
  10.8 0.1 pad_maximum_fusion
  10.9 22.5 %all_to_all.25 = bf16[8,8,9600]{2,0,1:T(8,128)(2,1)S(1)} all-to-all(bf16[8,8,9600]{2,0,1:T(8,128)(2,1)S(1)} %pad_maximum_fusion), channel_id=1, replica_groups=mesh['seq'=16,'head'=8] {'head'}, dimensions={1} | all-to-all | bytes 2457600 | tf_op jit(solution)/shard_map/all_to_all | solution.py:35
  33.4 0.9 slice.52
  34.3 0.0 all-gather.3.cloned.1.call-update
  34.3 0.0 all-gather.5.cloned.1.call-start
  34.3 0.8 slice.55
  35.2 0.0 all-gather.5.cloned.1.call-update
  35.2 1.0 broadcast_in_dim.37
  36.2 8.3 %all-to-all-start.1 = ((bf16[16,64,384]{2,1,0:T(8,128)(2,1)}), bf16[16,64,384]{2,1,0:T(8,128)(2,1)S(1)}, u32[]{:S(2)}, u32[]{:S(2)}) async-start(bf16[16,64,384]{2,1,0:T(8,128)(2,1)} %broadcast_in_dim.37), calls=%async_computation.1 | async-start | bytes 1572864 | tf_op jit(solution)/shard_map/all_to_all | solution.py:39
  44.5 0.0 copy-done.3
  44.5 0.1 iota_compare_fusion
  44.5 17.6 %all-to-all-done.1 = bf16[16,64,384]{2,1,0:T(8,128)(2,1)S(1)} async-done(((bf16[16,64,384]{2,1,0:T(8,128)(2,1)}), bf16[16,64,384]{2,1,0:T(8,128)(2,1)S(1)}, u32[]{:S(2)}, u32[]{:S(2)}) %all-to-all-start.1) | async-done | bytes 786464 | tf_op jit(solution)/shard_map/all_to_all | solution.py:39
  62.1 1.1 reshape.96
  63.2 7.4 %convert_bitcast_fusion = bf16[8,512,3,128]{1,3,0,2:T(8,128)(2,1)S(1)} fusion(bf16[8,512,1024]{2,1,0:T(8,128)(2,1)} %param.8, bf16[1024,3,128,1]{2,1,0,3:T(4,128)(2,1)} %bitcast.74), kind=kOutput, calls=%fused_computation.34 | convolution fusion | flops 3222798336 | bytes 12320768 | tf_op jit(solution)/shard_map/pld,dte->plte/dot_general | solution.py:70
  70.6 1.8 fusion.32
  72.3 10.8 %fusion.35 = (f32[8,2,512]{2,1,0:T(2,128)S(1)}, f32[8,2,512,512]{2,3,1,0:T(8,128)}) fusion(pred[8,512]{1,0:T(8,128)(4,1)S(1)} %iota_compare_fusion, bf16[8,512,2,64]{1,3,2,0:T(8,128)(2,1)} %bitcast.77, bf16[8,512,2,64]{1,3,2,0:T(8,128)(2,1)} %bitcast.76), kind=kOutput, calls=%fused_computation.64 | convolution fusion | flops 553648640 | bytes 18911232 | tf_op jit(solution)/shard_map/sub | solution.py:85
  83.1 9.0 %fusion.28 = bf16[8,512,2,64]{1,3,2,0:T(8,128)(2,1)} fusion(bf16[8,512,2,64]{1,3,2,0:T(8,128)(2,1)} %bitcast.75, f32[8,2,512,512]{2,3,1,0:T(8,128)} %get-tuple-element.22, f32[8,2,512]{2,1,0:T(2,128)S(1)} %get-tuple-element.21), kind=kOutput, calls=%fused_computation.43 | convolution fusion | flops 545783808 | bytes 18907136 | tf_op jit(solution)/shard_map/phqk,pkhd->pqhd/dot_general | solution.py:87
  92.2 0.0 copy-start.1
  92.2 0.0 copy-start.2
  92.2 3.9 %reshape.97 = bf16[8,8,64,128]{2,1,3,0:T(8,128)(2,1)} reshape(bf16[8,512,2,64]{1,3,2,0:T(8,128)(2,1)} %fusion.28) | data formatting | bytes 2097152 | tf_op jit(solution)/shard_map/reshape | solution.py:90
  96.1 3.4 %copy.28 = bf16[8,8,64,128]{3,2,1,0:T(8,128)(2,1)} copy(bf16[8,8,64,128]{2,0,3,1:T(8,128)(2,1)} %bitcast.69) | data formatting | bytes 2097152 | tf_op jit(solution)/shard_map/transpose | solution.py:93
  99.4 6.6 %all-to-all-start.2 = ((bf16[8,8,64,128]{3,2,1,0:T(8,128)(2,1)}), bf16[8,8,64,128]{3,2,1,0:T(8,128)(2,1)}, u32[]{:S(2)}, u32[]{:S(2)}) async-start(bf16[8,8,64,128]{3,2,1,0:T(8,128)(2,1)} %copy.28), calls=%async_computation.2 | async-start | bytes 2097152 | tf_op jit(solution)/shard_map/all_to_all | solution.py:94
  106.0 0.1 constant_dynamic-slice_fusion
  106.1 0.0 copy-done.1
  106.1 0.0 copy-done.2
  106.1 1.5 bitcast_select_fusion
  107.6 2.3 %copy.32 = bf16[8,512,128]{2,1,0:T(8,128)(2,1)} copy(bf16[8,512,128]{1,2,0:T(8,128)(2,1)} %get-tuple-element.13) | data formatting | bytes 2097152
  109.8 2.3 %copy.33 = bf16[8,512,128]{2,1,0:T(8,128)(2,1)} copy(bf16[8,512,128]{1,2,0:T(8,128)(2,1)} %get-tuple-element.12) | data formatting | bytes 2097152
  112.1 0.0 all-gather.3.cloned.1.call-done
  112.1 1.8 slice.53
  113.9 2.6 %copy.29 = bf16[1024,1024]{0,1:T(8,128)(2,1)} copy(bf16[1024,1024]{1,0:T(8,128)(2,1)S(1)} %slice.53) | data formatting | bytes 4194304 | tf_op jit(solution)/shard_map/slice | solution.py:43
  116.4 5.1 %all-to-all-done.2 = bf16[8,8,64,128]{3,2,1,0:T(8,128)(2,1)} async-done(((bf16[8,8,64,128]{3,2,1,0:T(8,128)(2,1)}), bf16[8,8,64,128]{3,2,1,0:T(8,128)(2,1)}, u32[]{:S(2)}, u32[]{:S(2)}) %all-to-all-start.2) | async-done | bytes 1048608 | tf_op jit(solution)/shard_map/all_to_all | solution.py:94
  121.5 0.0 copy-start
  121.5 3.7 %fusion.36 = (f32[8,64]{1,0:T(8,128)S(1)}, f32[8,64,1024]{2,1,0:T(8,128)S(1)}) fusion(bf16[8,8,64,128]{3,2,1,0:T(8,128)(2,1)} %all-to-all-done.2, bf16[1024,8,128,1]{0,2,3,1:T(8,128)(2,1)} %bitcast.73, bf16[8,512,1024]{2,1,0:T(8,128)(2,1)} %param.8, s32[]{:T(128)S(6)} %select_n.19), kind=kOutput, calls=%fused_computation.65 | convolution fusion | flops 1075314176 | bytes 6293508 | tf_op jit(solution)/shard_map/sprf,esf->pre/dot_general | solution.py:96
  125.2 0.3 multiply_reduce_fusion.1
  125.6 1.4 copy-done
  127.0 23.4 %fusion.4 = bf16[8,64,4096]{2,1,0:T(8,128)(2,1)} fusion(bf16[1024,5120]{1,0:T(8,128)(2,1)S(1)} %copy-done, f32[8,64,1024]{2,1,0:T(8,128)S(1)} %get-tuple-element.24, f32[1024]{0:T(1024)S(1)} %bitcast.82, f32[1024]{0:T(1024)S(1)} %bitcast.80, f32[8,64]{1,0:T(8,128)S(1)} %add_rsqrt_fusion.1, f32[8,64]{1,0:T(8,128)S(1)} %broadcast_multiply_fusion.1), kind=kOutput, calls=%fused_computation.8 | convolution fusion | flops 4433903616 | bytes 14696448 | tf_op jit(solution)/shard_map/pld,df->plf/dot_general | solution.py:104
  150.4 12.9 %all-gather.5.cloned.1.call-done = bf16[1024,4096]{1,0:T(8,128)(2,1)} async-done(((bf16[64,4096]{1,0:T(8,128)(2,1)}), bf16[1024,4096]{1,0:T(8,128)(2,1)}) %all-gather.5.cloned.1.call-update) | async-done | bytes 8388624 | tf_op jit(solution)/shard_map/all_gather | solution.py:45
  163.3 8.4 %fusion.37 = (f32[8,64]{1,0:T(8,128)S(1)}, f32[8,64,1024]{2,1,0:T(8,128)S(1)}) fusion(bf16[8,64,4096]{2,1,0:T(8,128)(2,1)} %fusion.4, bf16[1024,4096]{1,0:T(8,128)(2,1)} %all-gather.5.cloned.1.call-done, f32[1024]{0:T(1024)S(1)} %bitcast.83, f32[1024]{0:T(1024)S(1)} %bitcast.81, f32[8,64]{1,0:T(8,128)S(1)} %add_rsqrt_fusion.1, ...), kind=kOutput, calls=%fused_computation.66 | convolution fusion | flops 4299161088 | bytes 16791552 | tf_op jit(solution)/shard_map/plf,ef->ple/dot_general | solution.py:108
  171.7 0.3 multiply_reduce_fusion
  172.1 2.6 %select_convert_fusion = bf16[8,64,1024]{2,1,0:T(8,128)(2,1)} fusion(f32[8,64,1024]{2,1,0:T(8,128)S(1)} %get-tuple-element.26, f32[1024]{0:T(1024)S(1)} %bitcast.79, f32[1024]{0:T(1024)S(1)} %bitcast.78, f32[8,64]{1,0:T(8,128)S(1)} %add_rsqrt_fusion, f32[8,64]{1,0:T(8,128)S(1)} %broadcast_multiply_fusion, pred[8,64]{1,0:T(8,128)(4,1)S(1)} %constant_dynamic-slice_fusion), kind=kLoop, calls=%fused_computation.36 | loop fusion | flops 3145728 | bytes 3158528 | tf_op jit(solution)/shard_map/convert_element_type | solution.py:111
  (8 shorter events, 0.1 us)
Async XLA Ops:
  7.2 37.3 %copy-start.3 = (s32[8]{0:T(128)S(1)}, s32[8]{0:T(128)}, u32[]{:S(2)}) copy-start(s32[8]{0:T(128)} %param.9) | copy-start | bytes 100
  7.2 104.9 %all-gather.3.cloned.1.call-start = ((), (), s32[]{:S(2)}) async-start(), calls=%async_computation.3 | async-start | bytes 11141120 | tf_op jit(solution)/shard_map/all_gather | solution.py:42
  34.3 129.0 %all-gather.5.cloned.1.call-start = ((), (), s32[]{:S(2)}) async-start(), calls=%async_computation.4 | async-start | bytes 8912896 | tf_op jit(solution)/shard_map/all_gather | solution.py:45
  36.2 25.9 %all-to-all-start.1 = ((bf16[16,64,384]{2,1,0:T(8,128)(2,1)}), bf16[16,64,384]{2,1,0:T(8,128)(2,1)S(1)}, u32[]{:S(2)}, u32[]{:S(2)}) async-start(bf16[16,64,384]{2,1,0:T(8,128)(2,1)} %broadcast_in_dim.37), calls=%async_computation.1 | async-start | bytes 1572864 | tf_op jit(solution)/shard_map/all_to_all | solution.py:39
  92.2 13.9 %copy-start.1 = (f32[2,1024]{1,0:T(2,128)S(1)}, f32[2,1024]{1,0:T(2,128)}, u32[]{:S(2)}) copy-start(f32[2,1024]{1,0:T(2,128)} %param.14) | copy-start | bytes 24580
  92.2 13.9 %copy-start.2 = (f32[2,1024]{1,0:T(2,128)S(1)}, f32[2,1024]{1,0:T(2,128)}, u32[]{:S(2)}) copy-start(f32[2,1024]{1,0:T(2,128)} %param.15) | copy-start | bytes 24580
  99.4 22.1 %all-to-all-start.2 = ((bf16[8,8,64,128]{3,2,1,0:T(8,128)(2,1)}), bf16[8,8,64,128]{3,2,1,0:T(8,128)(2,1)}, u32[]{:S(2)}, u32[]{:S(2)}) async-start(bf16[8,8,64,128]{3,2,1,0:T(8,128)(2,1)} %copy.28), calls=%async_computation.2 | async-start | bytes 2097152 | tf_op jit(solution)/shard_map/all_to_all | solution.py:94
  121.5 5.4 %copy-start = (bf16[1024,5120]{1,0:T(8,128)(2,1)S(1)}, bf16[1024,5120]{1,0:T(8,128)(2,1)}, u32[]{:S(2)}) copy-start(bf16[1024,5120]{1,0:T(8,128)(2,1)} %all-gather.3.cloned.1.call-done) | copy-start | bytes 31457284
Sparse Core Ops, SparseCore 0:
  34.4 72.0 all-gather.2
  108.2 55.0 all-gather.4
where the time goes:
time: 182 us; the launch traced here: 181 us
  matrix products  62.7 us (34%)
  waiting for transfers between devices  35.6 us (20%)
  local copies, waits for them, and re-layouts  23.2 us (13%)
  blocking collectives  22.5 us (12%)
  starting transfers between devices  14.9 us (8%)
  between operations  14.2 us (8%)
  other arithmetic  8.38 us (5%)
    dot_general x1, matrix products, encode_chunk(): jnp.einsum('pld,df->plf', normed_rows, up_weight, preferred_element_type=...  23.4 us
    all_to_all x1, blocking collectives, regroup_weights(): packed = lax.all_to_all(packed, 'head', 1, 0, tiled=True)  22.5 us
    all_to_all x1, waiting for transfers between devices, regroup_weights(): qkv_weight = lax.all_to_all(in_part, 'seq', 0, 0, tiled=True)  17.6 us
    all_gather x1, waiting for transfers between devices, regroup_weights(): lax.all_gather(packed[:, early_end:], 'seq', axis=0, tiled=True)  12.9 us
    sub x1, matrix products, encode_chunk(): raised = jnp.exp(scores - row_peak)  10.8 us
    dot_general x1, matrix products, encode_chunk(): jnp.einsum('phqk,pkhd->pqhd', weights, value_heads, preferred_element_typ...  9 us
    dot_general x1, matrix products, encode_chunk(): jnp.einsum('plf,ef->ple', hidden, down_weight_t, preferred_element_type=j...  8.42 us
    all_to_all x1, starting transfers between devices, regroup_weights(): qkv_weight = lax.all_to_all(in_part, 'seq', 0, 0, tiled=True)  8.29 us
  transfers between devices with their start and end apart: 4, of which 3 were waited for; matrix products, arithmetic and copies ran while one was open for 42% of the time, Pallas kernels for 0%

commit v1 on v0

--- a/solution.py
+++ b/solution.py
@@ -42,7 +42,10 @@
     early = lax.all_gather(packed[:, 3 * block_width : early_end], "seq", axis=0, tiled=True)
     proj_weight_t = early[:, :model_width]
     up_weight = early[:, model_width:]
-    down_weight_t = lax.all_gather(packed[:, early_end:], "seq", axis=0, tiled=True)
+    down_weight_t = jnp.concatenate(
+        lax.all_to_all(jnp.stack([packed[:, early_end:]] * lax.axis_size("seq")), "seq", 0, 0),
+        axis=0,
+    )
     return (qkv_weight, proj_weight_t, up_weight, down_weight_t)
 
 

time: 182 us -> 248 us (1.36)
  waiting for transfers between devices: 35.6 us -> 84.9 us
  starting transfers between devices: 14.9 us -> 23.6 us
  local copies, waits for them, and re-layouts: 23.2 us -> 29.5 us
    all_to_all x0 -> x1, waiting for transfers between devices: none -> 55.1 us  [regroup_weights(): lax.all_to_all(jnp.stack([packed[:, early_end:]] * lax.axis_size('seq')),...]
    all_gather x1 -> x0, waiting for transfers between devices: 12.9 us -> none  [regroup_weights(): lax.all_gather(packed[:, early_end:], 'seq', axis=0, tiled=True)]
    all_to_all x1, waiting for transfers between devices: 5.11 us -> 13.3 us  [encode_chunk(): context_blocks = lax.all_to_all(context_blocks, 'head', 0, 0, tiled=True)]
    all_to_all x0 -> x1, starting transfers between devices: none -> 7.42 us  [regroup_weights(): lax.all_to_all(jnp.stack([packed[:, early_end:]] * lax.axis_size('seq')),...]
    another operation x0 -> x1, local copies, waits for them, and re-layouts: none -> 5.34 us  [regroup_weights(): jnp.stack([packed[:, early_end:]] * lax.axis_size('seq'))]
    unnamed x10 -> x12, local copies, waits for them, and re-layouts: 5.91 us -> 5.74 us
  transfers between devices with their start and end apart: 4 -> 4, of which waited for: 3 -> 3; matrix products, arithmetic and copies ran while one was open for 42% -> 34% of each run, Pallas kernels for 0% -> 0%
where the time goes in v1:
time: 248 us; the launch traced here: 246 us
  waiting for transfers between devices  84.9 us (34%)
  matrix products  62.6 us (25%)
  local copies, waits for them, and re-layouts  29.5 us (12%)
  starting transfers between devices  23.6 us (10%)
  blocking collectives  22.5 us (9%)
  between operations  14.2 us (6%)
  other arithmetic  8.38 us (3%)
    all_to_all x1, waiting for transfers between devices, regroup_weights(): lax.all_to_all(jnp.stack([packed[:, early_end:]] * lax.axis_size('seq')),...  55.1 us
    dot_general x1, matrix products, encode_chunk(): jnp.einsum('pld,df->plf', normed_rows, up_weight, preferred_element_type=...  23.4 us
    all_to_all x1, blocking collectives, regroup_weights(): packed = lax.all_to_all(packed, 'head', 1, 0, tiled=True)  22.5 us
    all_to_all x1, waiting for transfers between devices, regroup_weights(): qkv_weight = lax.all_to_all(in_part, 'seq', 0, 0, tiled=True)  16.5 us
    all_to_all x1, waiting for transfers between devices, encode_chunk(): context_blocks = lax.all_to_all(context_blocks, 'head', 0, 0, tiled=True)  13.3 us
    sub x1, matrix products, encode_chunk(): raised = jnp.exp(scores - row_peak)  10.8 us
    dot_general x1, matrix products, encode_chunk(): jnp.einsum('phqk,pkhd->pqhd', weights, value_heads, preferred_element_typ...  8.99 us
    dot_general x1, matrix products, encode_chunk(): jnp.einsum('plf,ef->ple', hidden, down_weight_t, preferred_element_type=j...  8.41 us
  transfers between devices with their start and end apart: 4, of which 3 were waited for; matrix products, arithmetic and copies ran while one was open for 34% of the time, Pallas kernels for 0%

profile of v1, /device:TPU:25, one launch (start us, length us, event | category | flops | bytes accessed | tf_op | source)
XLA Modules:
  0.0 245.6 jit_solution(7026375357009473060)
XLA Ops:
  7.2 0.0 copy-start.4
  7.2 0.0 all-gather.2.cloned.1.call-start
  7.2 0.9 convert_bitcast_fusion.1
  8.1 0.9 convert_element_type.45
  9.0 0.8 convert_bitcast_fusion.3
  9.8 0.9 copy_bitcast_fusion
  10.7 0.1 broadcast_in_dim.36
  10.8 0.1 pad_maximum_fusion
  10.9 22.5 %all_to_all.30 = bf16[8,8,9600]{2,0,1:T(8,128)(2,1)S(1)} all-to-all(bf16[8,8,9600]{2,0,1:T(8,128)(2,1)S(1)} %pad_maximum_fusion), channel_id=1, replica_groups=mesh['seq'=16,'head'=8] {'head'}, dimensions={1} | all-to-all | bytes 2457600 | tf_op jit(solution)/shard_map/all_to_all | solution.py:35
  33.4 0.0 copy-start
  33.4 0.9 slice.52
  34.3 0.0 all-gather.2.cloned.1.call-update
  34.3 1.0 broadcast_in_dim.37
  35.3 8.3 %all-to-all-start.1 = ((bf16[16,64,384]{2,1,0:T(8,128)(2,1)}), bf16[16,64,384]{2,1,0:T(8,128)(2,1)S(1)}, u32[]{:S(2)}, u32[]{:S(2)}) async-start(bf16[16,64,384]{2,1,0:T(8,128)(2,1)} %broadcast_in_dim.37), calls=%async_computation.1 | async-start | bytes 1572864 | tf_op jit(solution)/shard_map/all_to_all | solution.py:39
  43.6 0.0 copy-done.4
  43.6 0.1 iota_compare_fusion
  43.7 16.5 %all-to-all-done.1 = bf16[16,64,384]{2,1,0:T(8,128)(2,1)S(1)} async-done(((bf16[16,64,384]{2,1,0:T(8,128)(2,1)}), bf16[16,64,384]{2,1,0:T(8,128)(2,1)S(1)}, u32[]{:S(2)}, u32[]{:S(2)}) %all-to-all-start.1) | async-done | bytes 786464 | tf_op jit(solution)/shard_map/all_to_all | solution.py:39
  60.2 1.1 reshape.101
  61.3 0.0 copy-done
  61.3 7.4 %convert_bitcast_fusion = bf16[8,512,3,128]{1,3,0,2:T(8,128)(2,1)S(1)} fusion(bf16[8,512,1024]{2,1,0:T(8,128)(2,1)} %param.8, bf16[1024,3,128,1]{2,1,0,3:T(4,128)(2,1)} %bitcast.71), kind=kOutput, calls=%fused_computation.32 | convolution fusion | flops 3222798336 | bytes 12320768 | tf_op jit(solution)/shard_map/pld,dte->plte/dot_general | solution.py:73
  68.6 1.8 fusion.28
  70.4 10.8 %fusion.31 = (f32[8,2,512]{2,1,0:T(2,128)S(1)}, f32[8,2,512,512]{2,3,1,0:T(8,128)}) fusion(pred[8,512]{1,0:T(8,128)(4,1)S(1)} %iota_compare_fusion, bf16[8,512,2,64]{1,3,2,0:T(8,128)(2,1)} %bitcast.74, bf16[8,512,2,64]{1,3,2,0:T(8,128)(2,1)} %bitcast.73), kind=kOutput, calls=%fused_computation.62 | convolution fusion | flops 553648640 | bytes 18911232 | tf_op jit(solution)/shard_map/sub | solution.py:88
  81.2 9.0 %fusion.24 = bf16[8,512,2,64]{1,3,2,0:T(8,128)(2,1)} fusion(bf16[8,512,2,64]{1,3,2,0:T(8,128)(2,1)} %bitcast.72, f32[8,2,512,512]{2,3,1,0:T(8,128)} %get-tuple-element.22, f32[8,2,512]{2,1,0:T(2,128)S(1)} %get-tuple-element.21), kind=kOutput, calls=%fused_computation.41 | convolution fusion | flops 545783808 | bytes 18907136 | tf_op jit(solution)/shard_map/phqk,pkhd->pqhd/dot_general | solution.py:90
  90.2 3.9 %reshape.102 = bf16[8,8,64,128]{2,1,3,0:T(8,128)(2,1)} reshape(bf16[8,512,2,64]{1,3,2,0:T(8,128)(2,1)} %fusion.24) | data formatting | bytes 2097152 | tf_op jit(solution)/shard_map/reshape | solution.py:93
  94.1 3.4 %copy.28 = bf16[8,8,64,128]{3,2,1,0:T(8,128)(2,1)} copy(bf16[8,8,64,128]{2,0,3,1:T(8,128)(2,1)} %bitcast.66) | data formatting | bytes 2097152 | tf_op jit(solution)/shard_map/transpose | solution.py:96
  97.5 7.9 %all-to-all-start.2 = ((bf16[8,8,64,128]{3,2,1,0:T(8,128)(2,1)}), bf16[8,8,64,128]{3,2,1,0:T(8,128)(2,1)}, u32[]{:S(2)}, u32[]{:S(2)}) async-start(bf16[8,8,64,128]{3,2,1,0:T(8,128)(2,1)} %copy.28), calls=%async_computation.2 | async-start | bytes 2097152 | tf_op jit(solution)/shard_map/all_to_all | solution.py:97
  105.3 1.9 slice.55
  107.2 13.3 %all-to-all-done.2 = bf16[8,8,64,128]{3,2,1,0:T(8,128)(2,1)} async-done(((bf16[8,8,64,128]{3,2,1,0:T(8,128)(2,1)}), bf16[8,8,64,128]{3,2,1,0:T(8,128)(2,1)}, u32[]{:S(2)}, u32[]{:S(2)}) %all-to-all-start.2) | async-done | bytes 1048608 | tf_op jit(solution)/shard_map/all_to_all | solution.py:97
  120.5 5.3 %stack.2 = bf16[16,64,4096]{2,1,0:T(8,128)(2,1)} broadcast(bf16[64,4096]{1,0:T(8,128)(2,1)} %slice.55), dimensions={1,2} | broadcast | bytes 8912896 | tf_op jit(solution)/shard_map/stack | solution.py:46
  125.8 0.0 copy-start.2
  125.8 0.0 copy-start.3
  125.8 7.4 %all-to-all-start.3 = ((bf16[16,64,4096]{2,1,0:T(8,128)(2,1)}), bf16[16,64,4096]{2,1,0:T(8,128)(2,1)}, u32[]{:S(2)}, u32[]{:S(2)}) async-start(bf16[16,64,4096]{2,1,0:T(8,128)(2,1)} %stack.2), calls=%async_computation.3 | async-start | bytes 16777216 | tf_op jit(solution)/shard_map/all_to_all | solution.py:46
  133.2 0.1 constant_dynamic-slice_fusion
  133.3 0.0 copy-done.2
  133.3 0.0 copy-done.3
  133.4 1.5 bitcast_select_fusion
  134.8 2.3 copy.32
  137.1 2.3 copy.33
  139.3 0.0 all-gather.2.cloned.1.call-done
  139.3 1.8 slice.53
  141.1 2.6 %copy.29 = bf16[1024,1024]{0,1:T(8,128)(2,1)} copy(bf16[1024,1024]{1,0:T(8,128)(2,1)S(1)} %slice.53) | data formatting | bytes 4194304 | tf_op jit(solution)/shard_map/slice | solution.py:43
  143.7 0.0 copy-start.1
  143.7 3.7 %fusion.32 = (f32[8,64]{1,0:T(8,128)S(1)}, f32[8,64,1024]{2,1,0:T(8,128)S(1)}) fusion(bf16[8,8,64,128]{3,2,1,0:T(8,128)(2,1)} %all-to-all-done.2, bf16[1024,8,128,1]{0,2,3,1:T(8,128)(2,1)} %bitcast.70, bf16[8,512,1024]{2,1,0:T(8,128)(2,1)} %param.8, s32[]{:T(128)S(6)} %select_n.19), kind=kOutput, calls=%fused_computation.63 | convolution fusion | flops 1075314176 | bytes 6293508 | tf_op jit(solution)/shard_map/sprf,esf->pre/dot_general | solution.py:99
  147.3 0.3 multiply_reduce_fusion.1
  147.7 1.2 copy-done.1
  148.9 23.4 %fusion.4 = bf16[8,64,4096]{2,1,0:T(8,128)(2,1)} fusion(bf16[1024,5120]{1,0:T(8,128)(2,1)S(1)} %copy-done.1, f32[8,64,1024]{2,1,0:T(8,128)S(1)} %get-tuple-element.24, f32[1024]{0:T(1024)S(1)} %bitcast.79, f32[1024]{0:T(1024)S(1)} %bitcast.77, f32[8,64]{1,0:T(8,128)S(1)} %add_rsqrt_fusion.1, f32[8,64]{1,0:T(8,128)S(1)} %broadcast_multiply_fusion.1), kind=kOutput, calls=%fused_computation.8 | convolution fusion | flops 4433903616 | bytes 14696448 | tf_op jit(solution)/shard_map/pld,df->plf/dot_general | solution.py:107
  172.3 55.1 %all-to-all-done.3 = bf16[16,64,4096]{2,1,0:T(8,128)(2,1)} async-done(((bf16[16,64,4096]{2,1,0:T(8,128)(2,1)}), bf16[16,64,4096]{2,1,0:T(8,128)(2,1)}, u32[]{:S(2)}, u32[]{:S(2)}) %all-to-all-start.3) | async-done | bytes 8388640 | tf_op jit(solution)/shard_map/all_to_all | solution.py:46
  227.4 8.4 %fusion.33 = (f32[8,64]{1,0:T(8,128)S(1)}, f32[8,64,1024]{2,1,0:T(8,128)S(1)}) fusion(bf16[8,64,4096]{2,1,0:T(8,128)(2,1)} %fusion.4, bf16[1024,4096,1]{1,0,2:T(8,128)(2,1)} %bitcast.25, f32[1024]{0:T(1024)S(1)} %bitcast.80, f32[1024]{0:T(1024)S(1)} %bitcast.78, f32[8,64]{1,0:T(8,128)S(1)} %add_rsqrt_fusion.1, f32[8,64,1024]{2,1,0:T(8,128)S(1)} %get-tuple-element.24, ...), kind=kOutput, calls=%fused_computation.64 | convolution fusion | flops 4299161088 | bytes 16791552 | tf_op jit(solution)/shard_map/plf,ef->ple/dot_general | solution.py:111
  235.8 0.3 multiply_reduce_fusion
  236.2 2.6 %select_convert_fusion = bf16[8,64,1024]{2,1,0:T(8,128)(2,1)} fusion(f32[8,64,1024]{2,1,0:T(8,128)S(1)} %get-tuple-element.26, f32[1024]{0:T(1024)S(1)} %bitcast.76, f32[1024]{0:T(1024)S(1)} %bitcast.75, f32[8,64]{1,0:T(8,128)S(1)} %add_rsqrt_fusion, f32[8,64]{1,0:T(8,128)S(1)} %broadcast_multiply_fusion, pred[8,64]{1,0:T(8,128)(4,1)S(1)} %constant_dynamic-slice_fusion), kind=kLoop, calls=%fused_computation.34 | loop fusion | flops 3145728 | bytes 3158528 | tf_op jit(solution)/shard_map/convert_element_type | solution.py:114
  (8 shorter events, 0.1 us)
Async XLA Ops:
  7.2 36.5 %copy-start.4 = (s32[8]{0:T(128)S(1)}, s32[8]{0:T(128)}, u32[]{:S(2)}) copy-start(s32[8]{0:T(128)} %param.9) | copy-start | bytes 100
  7.2 132.2 %all-gather.2.cloned.1.call-start = ((), (), s32[]{:S(2)}) async-start(), calls=%async_computation.4 | async-start | bytes 11141120 | tf_op jit(solution)/shard_map/all_gather | solution.py:42
  33.4 27.9 %copy-start = (bf16[8,8,9600]{2,0,1:T(8,128)(2,1)}, bf16[8,8,9600]{2,0,1:T(8,128)(2,1)S(1)}, u32[]{:S(2)}) copy-start(bf16[8,8,9600]{2,0,1:T(8,128)(2,1)S(1)} %all_to_all.30) | copy-start | bytes 3686404
  35.3 24.9 %all-to-all-start.1 = ((bf16[16,64,384]{2,1,0:T(8,128)(2,1)}), bf16[16,64,384]{2,1,0:T(8,128)(2,1)S(1)}, u32[]{:S(2)}, u32[]{:S(2)}) async-start(bf16[16,64,384]{2,1,0:T(8,128)(2,1)} %broadcast_in_dim.37), calls=%async_computation.1 | async-start | bytes 1572864 | tf_op jit(solution)/shard_map/all_to_all | solution.py:39
  97.5 23.0 %all-to-all-start.2 = ((bf16[8,8,64,128]{3,2,1,0:T(8,128)(2,1)}), bf16[8,8,64,128]{3,2,1,0:T(8,128)(2,1)}, u32[]{:S(2)}, u32[]{:S(2)}) async-start(bf16[8,8,64,128]{3,2,1,0:T(8,128)(2,1)} %copy.28), calls=%async_computation.2 | async-start | bytes 2097152 | tf_op jit(solution)/shard_map/all_to_all | solution.py:97
  125.8 7.5 %copy-start.2 = (f32[2,1024]{1,0:T(2,128)S(1)}, f32[2,1024]{1,0:T(2,128)}, u32[]{:S(2)}) copy-start(f32[2,1024]{1,0:T(2,128)} %param.14) | copy-start | bytes 24580
  125.8 7.5 %copy-start.3 = (f32[2,1024]{1,0:T(2,128)S(1)}, f32[2,1024]{1,0:T(2,128)}, u32[]{:S(2)}) copy-start(f32[2,1024]{1,0:T(2,128)} %param.15) | copy-start | bytes 24580
  125.8 101.6 %all-to-all-start.3 = ((bf16[16,64,4096]{2,1,0:T(8,128)(2,1)}), bf16[16,64,4096]{2,1,0:T(8,128)(2,1)}, u32[]{:S(2)}, u32[]{:S(2)}) async-start(bf16[16,64,4096]{2,1,0:T(8,128)(2,1)} %stack.2), calls=%async_computation.3 | async-start | bytes 16777216 | tf_op jit(solution)/shard_map/all_to_all | solution.py:46
  143.7 5.2 %copy-start.1 = (bf16[1024,5120]{1,0:T(8,128)(2,1)S(1)}, bf16[1024,5120]{1,0:T(8,128)(2,1)}, u32[]{:S(2)}) copy-start(bf16[1024,5120]{1,0:T(8,128)(2,1)} %all-gather.2.cloned.1.call-done) | copy-start | bytes 31457284
Sparse Core Ops, SparseCore 0:
  34.4 71.1 all-gather.1
